TPU v7x, 256 devices: a whole 4x4x8 slice. The times are simulated.
256 devices in a mesh: row: 16 (over x, y), col: 16 (over z, core).
Axes of the slice: x: 4, y: 4, z: 8, core: 2. Of those that a mesh axis runs over, the one named last changes fastest.
Arguments:
- features: bfloat16 [65536, 256], P(('col', 'row')), may hold values from -6 to 6
- cotangent: bfloat16 [65536, 256], P(('row', 'col')), may hold values from -1.5 to 1.5
- degrees: int32 [65536], P(('row', 'col')), may hold values from 8 to 40
- weight: bfloat16 [256, 256], replicated, may hold values from -0.375 to 0.375
- tile_rows: int32 [16, 16, 256], P('row', 'col'), may hold values from 0 to 31
- tile_cols: int32 [16, 16, 256], P('row', 'col'), may hold values from 0 to 31
- tile_bits: int32 [16, 16, 256, 16, 128], P('row', 'col'), may hold values from 0 to 255, as said below
- tile_count: int32 [16, 16], P('row', 'col'), may hold values from 16 to 256, as said below
Outputs:
- output: bfloat16 [65536, 256], P(('row', 'col'))
- weight_grad: float32 [256, 256], replicated
- input_grad: bfloat16 [65536, 256], P(('col', 'row'))
Inputs may be any that keep to these rules, and one draw needn't show every extreme that they name: `tile_bits`: each word holds 8 entries of 0 or 1 in its low bits; tiles at the same position may repeat and then add. `tile_count`: some device has all 256 slots live and some device 256 // 16.
All inputs are finite; a program needn't handle non-finite values.
Results may differ from a plain program's by a relative error of at most 0.024.
Values may be sent and summed in bfloat16 or wider, within the bound.
No kernel may reach another device: no remote copies, remote signals or barrier semaphores. Data moves between devices by JAX's collectives and lax.ppermute only.
A program may use at most 64 MiB of HBM per device.

v0:
```python
import math
import jax
import jax.numpy as jnp
from jax import lax
from jax.sharding import PartitionSpec as P


def unpack(packed):
    shifts = jnp.arange(8, dtype=jnp.int32)
    flags = jnp.right_shift(packed[:, :, None, :], shifts[None, None, :, None]) & 1
    return flags.reshape(packed.shape[0], packed.shape[1] * 8, packed.shape[2])


def sweep_tiles(packed, row_ids, col_ids, live_count, source, tile_offset, out_tiles, forward):
    tile_size = packed.shape[-1]
    feature_width = source.shape[-1]
    block_size = math.gcd(packed.shape[0], 32)

    def one_block(position, totals):
        offset = position * block_size
        block_bits = lax.dynamic_slice_in_dim(packed, offset, block_size, 0)
        block_rows = lax.dynamic_slice_in_dim(row_ids, offset, block_size, 0)
        block_cols = lax.dynamic_slice_in_dim(col_ids, offset, block_size, 0)
        if forward:
            target = block_rows - tile_offset
        else:
            target = block_cols - tile_offset
        inside = (target >= 0) & (target < out_tiles)
        live_mask = (offset + jnp.arange(block_size, dtype=jnp.int32) < live_count) & inside
        placed = jnp.clip(target, 0, out_tiles - 1)
        pattern = (unpack(block_bits) * live_mask.astype(jnp.int32)[:, None, None]).astype(
            jnp.bfloat16
        )
        if forward:
            product = jnp.einsum(
                "bji,bjf->bif", pattern, source[block_cols], preferred_element_type=jnp.float32
            )
        else:
            product = jnp.einsum(
                "bji,bif->bjf", pattern, source[block_rows], preferred_element_type=jnp.float32
            )
        return totals.at[placed].add(product)

    initial = jnp.zeros((out_tiles, tile_size, feature_width), jnp.float32)
    blocks_used = packed.shape[0] // block_size
    return lax.fori_loop(0, blocks_used, one_block, initial)


def forward_pass(features, degrees, weight, packed, row_ids, col_ids, live_count):
    tile_size = packed.shape[-1]
    width = features.shape[-1]
    gathered = lax.all_gather(features, "row", axis=0, tiled=True)
    source = gathered.reshape(-1, tile_size, width)
    out_tiles = features.shape[0] * lax.axis_size("col") // tile_size
    partial_value = sweep_tiles(packed, row_ids, col_ids, live_count, source, 0, out_tiles, True)
    summed = lax.psum_scatter(
        partial_value.reshape(-1, width).astype(jnp.bfloat16),
        "col",
        scatter_dimension=0,
        tiled=True,
    ).astype(jnp.float32)
    aggregated = (summed / degrees[:, None].astype(jnp.float32)).astype(jnp.bfloat16)
    output = jnp.dot(aggregated, weight, preferred_element_type=jnp.float32).astype(jnp.bfloat16)
    return (aggregated, output)


def backward_pass(cotangent, degrees, weight, packed, row_ids, col_ids, live_count):
    tile_size = packed.shape[-1]
    width = cotangent.shape[-1]
    scaled = (cotangent.astype(jnp.float32) / degrees[:, None].astype(jnp.float32)).astype(
        jnp.bfloat16
    )
    gathered = lax.all_gather(scaled, "col", axis=0, tiled=True)
    source = gathered.reshape(-1, tile_size, width)
    out_tiles = cotangent.shape[0] * lax.axis_size("row") // tile_size
    partial_value = sweep_tiles(packed, row_ids, col_ids, live_count, source, 0, out_tiles, False)
    summed = lax.psum_scatter(
        partial_value.reshape(-1, width).astype(jnp.bfloat16),
        "row",
        scatter_dimension=0,
        tiled=True,
    )
    return jnp.dot(summed, weight.T, preferred_element_type=jnp.float32).astype(jnp.bfloat16)


def per_device(features, cotangent, degrees, weight, tile_rows, tile_cols, tile_bits, tile_count):
    packed = tile_bits[0, 0]
    row_ids = tile_rows[0, 0]
    col_ids = tile_cols[0, 0]
    live_count = tile_count[0, 0]
    aggregated, output = forward_pass(
        features, degrees, weight, packed, row_ids, col_ids, live_count
    )
    input_grad = backward_pass(cotangent, degrees, weight, packed, row_ids, col_ids, live_count)
    local_term = lax.dot_general(
        aggregated, cotangent, (((0,), (0,)), ((), ())), preferred_element_type=jnp.float32
    )
    weight_grad = lax.psum(local_term, ("row", "col"))
    return (output, weight_grad, input_grad)


def solution(mesh):
    placed = (
        P(("col", "row"), None),
        P(("row", "col"), None),
        P(("row", "col")),
        P(),
        P("row", "col", None),
        P("row", "col", None),
        P("row", "col", None, None, None),
        P("row", "col"),
    )
    return jax.shard_map(
        per_device,
        mesh=mesh,
        in_specs=placed,
        out_specs=(P(("row", "col"), None), P(), P(("col", "row"), None)),
        check_vma=False,
    )
```

profile of v0, /device:TPU:2, one launch (start us, length us, event | category | flops | bytes accessed | tf_op | source)
XLA Modules:
  0.0 690.2 jit_solution(7609712674612229882)
XLA Ops:
  10.4 52.7 %all-gather.3.cloned.1.call-done = bf16[4096,256]{1,0:T(8,128)(2,1)} async-done(((bf16[256,256]{1,0:T(8,128)(2,1)}), bf16[4096,256]{1,0:T(8,128)(2,1)}) %all-gather.3.cloned.1.call-update) | async-done | bytes 2097168 | tf_op jit(solution)/shard_map/all_gather | solution.py:52
  65.5 136.1 %while.26 = (s32[]{:T(128)}, f32[32,128,256]{2,1,0:T(8,128)}, s32[256]{0:T(256)S(1)}, s32[256,16,128]{2,1,0:T(8,128)}, s32[]{:T(128)}, /*index=5*/s32[256]{0:T(2...) while((s32[]{:T(128)}, f32[32,128,256]{2,1,0:T(8,128)}, ...), condition=%wide.region_2.3_spmd, body=%wide.region_0.2_spmd.sunk | while | flops 271582656 | bytes 23862704 | solution.py:46
  72.6 10.0 %scatter_fusion = f32[32,128,256]{2,1,0:T(8,128)} fusion(f32[32,128,256]{2,1,0:T(8,128)} %get-tuple-element.398, s32[32]{0:T(128)S(1)} %get-tuple-element.375, f32[32,128,256]{2,1,0:T(8,128)} %fusion.35), kind=kCustom, calls=%fused_computation.2.clone.1 | custom fusion | flops 1048576 | bytes 12583040 | tf_op jit(solution)/shard_map/while/body/eval_jaxpr/scatter-add | solution.py:42
  89.7 10.0 %scatter_fusion = f32[32,128,256]{2,1,0:T(8,128)} fusion(f32[32,128,256]{2,1,0:T(8,128)} %get-tuple-element.398, s32[32]{0:T(128)S(1)} %get-tuple-element.375, f32[32,128,256]{2,1,0:T(8,128)} %fusion.35), kind=kCustom, calls=%fused_computation.2.clone.1 | custom fusion | flops 1048576 | bytes 12583040 | tf_op jit(solution)/shard_map/while/body/eval_jaxpr/scatter-add | solution.py:42
  106.8 9.8 %scatter_fusion = f32[32,128,256]{2,1,0:T(8,128)} fusion(f32[32,128,256]{2,1,0:T(8,128)} %get-tuple-element.398, s32[32]{0:T(128)S(1)} %get-tuple-element.375, f32[32,128,256]{2,1,0:T(8,128)} %fusion.35), kind=kCustom, calls=%fused_computation.2.clone.1 | custom fusion | flops 1048576 | bytes 12583040 | tf_op jit(solution)/shard_map/while/body/eval_jaxpr/scatter-add | solution.py:42
  123.6 9.9 %scatter_fusion = f32[32,128,256]{2,1,0:T(8,128)} fusion(f32[32,128,256]{2,1,0:T(8,128)} %get-tuple-element.398, s32[32]{0:T(128)S(1)} %get-tuple-element.375, f32[32,128,256]{2,1,0:T(8,128)} %fusion.35), kind=kCustom, calls=%fused_computation.2.clone.1 | custom fusion | flops 1048576 | bytes 12583040 | tf_op jit(solution)/shard_map/while/body/eval_jaxpr/scatter-add | solution.py:42
  140.6 9.9 %scatter_fusion = f32[32,128,256]{2,1,0:T(8,128)} fusion(f32[32,128,256]{2,1,0:T(8,128)} %get-tuple-element.398, s32[32]{0:T(128)S(1)} %get-tuple-element.375, f32[32,128,256]{2,1,0:T(8,128)} %fusion.35), kind=kCustom, calls=%fused_computation.2.clone.1 | custom fusion | flops 1048576 | bytes 12583040 | tf_op jit(solution)/shard_map/while/body/eval_jaxpr/scatter-add | solution.py:42
  157.5 10.0 %scatter_fusion = f32[32,128,256]{2,1,0:T(8,128)} fusion(f32[32,128,256]{2,1,0:T(8,128)} %get-tuple-element.398, s32[32]{0:T(128)S(1)} %get-tuple-element.375, f32[32,128,256]{2,1,0:T(8,128)} %fusion.35), kind=kCustom, calls=%fused_computation.2.clone.1 | custom fusion | flops 1048576 | bytes 12583040 | tf_op jit(solution)/shard_map/while/body/eval_jaxpr/scatter-add | solution.py:42
  171.7 2.9 fusion.35
  174.6 10.0 %scatter_fusion = f32[32,128,256]{2,1,0:T(8,128)} fusion(f32[32,128,256]{2,1,0:T(8,128)} %get-tuple-element.398, s32[32]{0:T(128)S(1)} %get-tuple-element.375, f32[32,128,256]{2,1,0:T(8,128)} %fusion.35), kind=kCustom, calls=%fused_computation.2.clone.1 | custom fusion | flops 1048576 | bytes 12583040 | tf_op jit(solution)/shard_map/while/body/eval_jaxpr/scatter-add | solution.py:42
  191.7 9.9 %scatter_fusion = f32[32,128,256]{2,1,0:T(8,128)} fusion(f32[32,128,256]{2,1,0:T(8,128)} %get-tuple-element.398, s32[32]{0:T(128)S(1)} %get-tuple-element.375, f32[32,128,256]{2,1,0:T(8,128)} %fusion.35), kind=kCustom, calls=%fused_computation.2.clone.1 | custom fusion | flops 1048576 | bytes 12583040 | tf_op jit(solution)/shard_map/while/body/eval_jaxpr/scatter-add | solution.py:42
  201.6 3.8 convert_element_type.63
  208.0 134.8 %while.27 = (s32[]{:T(128)}, f32[32,128,256]{2,1,0:T(8,128)}, s32[256]{0:T(256)S(1)}, s32[256,16,128]{2,1,0:T(8,128)}, s32[]{:T(128)}, /*index=5*/s32[256]{0:T(2...) while((s32[]{:T(128)}, f32[32,128,256]{2,1,0:T(8,128)}, ...), condition=%wide.region_7.8_spmd, body=%wide.region_5.7_spmd.sunk | while | flops 271582656 | bytes 23862704 | solution.py:46
  214.9 10.2 %scatter_fusion.1 = f32[32,128,256]{2,1,0:T(8,128)} fusion(f32[32,128,256]{2,1,0:T(8,128)} %get-tuple-element.431, s32[32]{0:T(128)S(1)} %get-tuple-element.384, f32[32,128,256]{2,1,0:T(8,128)} %fusion.38), kind=kCustom, calls=%fused_computation.3.clone.1 | custom fusion | flops 1048576 | bytes 12583040 | tf_op jit(solution)/shard_map/while/body/eval_jaxpr/scatter-add | solution.py:42
  232.0 9.8 %scatter_fusion.1 = f32[32,128,256]{2,1,0:T(8,128)} fusion(f32[32,128,256]{2,1,0:T(8,128)} %get-tuple-element.431, s32[32]{0:T(128)S(1)} %get-tuple-element.384, f32[32,128,256]{2,1,0:T(8,128)} %fusion.38), kind=kCustom, calls=%fused_computation.3.clone.1 | custom fusion | flops 1048576 | bytes 12583040 | tf_op jit(solution)/shard_map/while/body/eval_jaxpr/scatter-add | solution.py:42
  248.7 10.0 %scatter_fusion.1 = f32[32,128,256]{2,1,0:T(8,128)} fusion(f32[32,128,256]{2,1,0:T(8,128)} %get-tuple-element.431, s32[32]{0:T(128)S(1)} %get-tuple-element.384, f32[32,128,256]{2,1,0:T(8,128)} %fusion.38), kind=kCustom, calls=%fused_computation.3.clone.1 | custom fusion | flops 1048576 | bytes 12583040 | tf_op jit(solution)/shard_map/while/body/eval_jaxpr/scatter-add | solution.py:42
  265.5 9.9 %scatter_fusion.1 = f32[32,128,256]{2,1,0:T(8,128)} fusion(f32[32,128,256]{2,1,0:T(8,128)} %get-tuple-element.431, s32[32]{0:T(128)S(1)} %get-tuple-element.384, f32[32,128,256]{2,1,0:T(8,128)} %fusion.38), kind=kCustom, calls=%fused_computation.3.clone.1 | custom fusion | flops 1048576 | bytes 12583040 | tf_op jit(solution)/shard_map/while/body/eval_jaxpr/scatter-add | solution.py:42
  282.3 9.9 %scatter_fusion.1 = f32[32,128,256]{2,1,0:T(8,128)} fusion(f32[32,128,256]{2,1,0:T(8,128)} %get-tuple-element.431, s32[32]{0:T(128)S(1)} %get-tuple-element.384, f32[32,128,256]{2,1,0:T(8,128)} %fusion.38), kind=kCustom, calls=%fused_computation.3.clone.1 | custom fusion | flops 1048576 | bytes 12583040 | tf_op jit(solution)/shard_map/while/body/eval_jaxpr/scatter-add | solution.py:42
  299.0 10.0 %scatter_fusion.1 = f32[32,128,256]{2,1,0:T(8,128)} fusion(f32[32,128,256]{2,1,0:T(8,128)} %get-tuple-element.431, s32[32]{0:T(128)S(1)} %get-tuple-element.384, f32[32,128,256]{2,1,0:T(8,128)} %fusion.38), kind=kCustom, calls=%fused_computation.3.clone.1 | custom fusion | flops 1048576 | bytes 12583040 | tf_op jit(solution)/shard_map/while/body/eval_jaxpr/scatter-add | solution.py:42
  315.9 10.1 %scatter_fusion.1 = f32[32,128,256]{2,1,0:T(8,128)} fusion(f32[32,128,256]{2,1,0:T(8,128)} %get-tuple-element.431, s32[32]{0:T(128)S(1)} %get-tuple-element.384, f32[32,128,256]{2,1,0:T(8,128)} %fusion.38), kind=kCustom, calls=%fused_computation.3.clone.1 | custom fusion | flops 1048576 | bytes 12583040 | tf_op jit(solution)/shard_map/while/body/eval_jaxpr/scatter-add | solution.py:42
  332.8 10.0 %scatter_fusion.1 = f32[32,128,256]{2,1,0:T(8,128)} fusion(f32[32,128,256]{2,1,0:T(8,128)} %get-tuple-element.431, s32[32]{0:T(128)S(1)} %get-tuple-element.384, f32[32,128,256]{2,1,0:T(8,128)} %fusion.38), kind=kCustom, calls=%fused_computation.3.clone.1 | custom fusion | flops 1048576 | bytes 12583040 | tf_op jit(solution)/shard_map/while/body/eval_jaxpr/scatter-add | solution.py:42
  342.9 3.8 convert_element_type.71
  351.4 73.8 %reduce-scatter.5.cloned.1.call-done = bf16[256,256]{1,0:T(8,128)(2,1)} async-done(((bf16[4096,256]{1,0:T(8,128)(2,1)}), bf16[256,256]{1,0:T(8,128)(2,1)}) %reduce-scatter.5.cloned.1.call-update) | async-done | bytes 131088 | tf_op jit(solution)/shard_map/reduce_scatter | solution.py:77
  426.9 255.1 %all-reduce.2.cloned.1.call-done = f32[256,256]{1,0:T(8,128)} async-done(((f32[256,256]{1,0:T(8,128)}), f32[256,256]{1,0:T(8,128)}) %all-reduce.2.cloned.1.call-update) | async-done | bytes 262160 | tf_op jit(solution)/shard_map/psum | solution.py:98
  (155 shorter events, 124.4 us)
Async XLA Ops:
  7.2 342.4 %copy-start = (bf16[256,256]{1,0:T(8,128)(2,1)S(1)}, bf16[256,256]{1,0:T(8,128)(2,1)}, u32[]{:S(2)}) copy-start(bf16[256,256]{1,0:T(8,128)(2,1)} %param.15) | copy-start | bytes 393220
  7.2 55.9 %all-gather.3.cloned.1.call-start = ((), (), s32[]{:S(2)}) async-start(), calls=%async_computation.2 | async-start | bytes 2228224 | tf_op jit(solution)/shard_map/all_gather | solution.py:52
  7.9 197.6 %all-gather.5.cloned.1.call-start = ((), (), s32[]{:S(2)}) async-start(), calls=%async_computation.5 | async-start | bytes 2228224 | tf_op jit(solution)/shard_map/all_gather | solution.py:73
  10.3 336.5 %reduce-scatter.3.cloned.1.call-start = ((), (), s32[]{:S(2)}) async-start(), calls=%async_computation.3 | async-start | bytes 2228224 | tf_op jit(solution)/shard_map/reduce_scatter | solution.py:56
  63.1 2.5 copy-start.2
  63.1 2.5 copy-start.3
  205.5 219.7 %reduce-scatter.5.cloned.1.call-start = ((), (), s32[]{:S(2)}) async-start(), calls=%async_computation.6 | async-start | bytes 2228224 | tf_op jit(solution)/shard_map/reduce_scatter | solution.py:77
  346.7 0.9 copy-start.1
  346.7 335.2 %all-reduce.2.cloned.1.call-start = ((), (), s32[]{:S(2)}) async-start(), calls=%async_computation.4 | async-start | bytes 524288 | tf_op jit(solution)/shard_map/psum | solution.py:98
Sparse Core Ops, SparseCore 0:
  10.4 52.5 all-gather.2
  65.5 39.5 all-gather.4
  205.6 59.0 reduce-scatter.2
  346.9 78.2 reduce-scatter.4
  431.9 250.0 all-reduce.1
where the time goes:
time: 692 us; the launch traced here: 690 us
  waiting for transfers between devices  382 us (55%)
  other arithmetic  182 us (26%)
  local copies, waits for them, and re-layouts  60.8 us (9%)
  matrix products  50.3 us (7%)
  between operations  13.8 us (2%)
    psum x1, waiting for transfers between devices, per_device(): weight_grad = lax.psum(local_term, ('row', 'col'))  255 us
    scatter-add x16, other arithmetic, one_block(): return totals.at[placed].add(product)  159 us
    reduce_scatter x1, waiting for transfers between devices, backward_pass(): lax.psum_scatter(partial_value.reshape(-1, width).astype(jnp.bfloat16), '...  73.8 us
    all_gather x1, waiting for transfers between devices, forward_pass(): gathered = lax.all_gather(features, 'row', axis=0, tiled=True)  52.7 us
    dot_general x8, matrix products, one_block(): jnp.einsum('bji,bjf->bif', pattern, source[block_cols], preferred_element...  23.2 us
    dot_general x8, matrix products, one_block(): jnp.einsum('bji,bif->bjf', pattern, source[block_rows], preferred_element...  21.6 us
    gather x8, local copies, waits for them, and re-layouts, one_block(): source[block_rows]  18.2 us
    gather x8, local copies, waits for them, and re-layouts, one_block(): source[block_cols]  18.2 us
  transfers between devices with their start and end apart: 5, of which 3 were waited for; matrix products, arithmetic and copies ran while one was open for 42% of the time, Pallas kernels for 0%

commit v1 on v0

--- a/solution.py
+++ b/solution.py
@@ -95,7 +95,7 @@
     local_term = lax.dot_general(
         aggregated, cotangent, (((0,), (0,)), ((), ())), preferred_element_type=jnp.float32
     )
-    weight_grad = lax.psum(local_term, ("row", "col"))
+    weight_grad = lax.psum(lax.psum(local_term, "col"), "row")
     return (output, weight_grad, input_grad)
 
 

time: 692 us -> 631 us (0.912)
  waiting for transfers between devices: 382 us -> 323 us
    psum x1 -> x2, waiting for transfers between devices: 255 us -> 94.1 us  [per_device(): weight_grad = lax.psum(lax.psum(local_term, 'col'), 'row')]
    reduce_scatter x1, waiting for transfers between devices: 0.02 us -> 57.5 us  [forward_pass(): lax.psum_scatter(partial_value.reshape(-1, width).astype(jnp.bfloat16), '...]
    all_gather x1, waiting for transfers between devices: 0.02 us -> 38.7 us  [backward_pass(): gathered = lax.all_gather(scaled, 'col', axis=0, tiled=True)]
  transfers between devices with their start and end apart: 5 -> 6, of which waited for: 3 -> 5; matrix products, arithmetic and copies ran while one was open for 42% -> 23% of each run, Pallas kernels for 0% -> 0%
where the time goes in v1:
time: 631 us; the launch traced here: 629 us
  waiting for transfers between devices  323 us (51%)
  other arithmetic  181 us (29%)
  local copies, waits for them, and re-layouts  60.8 us (10%)
  matrix products  49.6 us (8%)
  between operations  14.1 us (2%)
    scatter-add x16, other arithmetic, one_block(): return totals.at[placed].add(product)  159 us
    psum x2, waiting for transfers between devices, per_device(): weight_grad = lax.psum(lax.psum(local_term, 'col'), 'row')  94.1 us
    reduce_scatter x1, waiting for transfers between devices, backward_pass(): lax.psum_scatter(partial_value.reshape(-1, width).astype(jnp.bfloat16), '...  76.9 us
    reduce_scatter x1, waiting for transfers between devices, forward_pass(): lax.psum_scatter(partial_value.reshape(-1, width).astype(jnp.bfloat16), '...  57.5 us
    all_gather x1, waiting for transfers between devices, forward_pass(): gathered = lax.all_gather(features, 'row', axis=0, tiled=True)  55.1 us
    all_gather x1, waiting for transfers between devices, backward_pass(): gathered = lax.all_gather(scaled, 'col', axis=0, tiled=True)  38.7 us
    dot_general x8, matrix products, one_block(): jnp.einsum('bji,bjf->bif', pattern, source[block_cols], preferred_element...  23.3 us
    dot_general x8, matrix products, one_block(): jnp.einsum('bji,bif->bjf', pattern, source[block_rows], preferred_element...  21.7 us
  transfers between devices with their start and end apart: 6, of which 5 were waited for; matrix products, arithmetic and copies ran while one was open for 23% of the time, Pallas kernels for 0%

profile of v1, /device:TPU:2, one launch (start us, length us, event | category | flops | bytes accessed | tf_op | source)
XLA Modules:
  0.0 629.2 jit_solution(6512705900646291427)
XLA Ops:
  8.0 55.1 %all-gather.3.cloned.1.call-done = bf16[4096,256]{1,0:T(8,128)(2,1)} async-done(((bf16[256,256]{1,0:T(8,128)(2,1)}), bf16[4096,256]{1,0:T(8,128)(2,1)}) %all-gather.3.cloned.1.call-update) | async-done | bytes 2097168 | tf_op jit(solution)/shard_map/all_gather | solution.py:52
  65.5 136.1 %while.26 = (s32[]{:T(128)}, f32[32,128,256]{2,1,0:T(8,128)}, s32[256]{0:T(256)S(1)}, s32[256,16,128]{2,1,0:T(8,128)}, s32[]{:T(128)}, /*index=5*/s32[256]{0:T(2...) while((s32[]{:T(128)}, f32[32,128,256]{2,1,0:T(8,128)}, ...), condition=%wide.region_2.3_spmd, body=%wide.region_0.2_spmd.sunk | while | flops 271582656 | bytes 23862704 | solution.py:46
  72.6 10.0 %scatter_fusion = f32[32,128,256]{2,1,0:T(8,128)} fusion(f32[32,128,256]{2,1,0:T(8,128)} %get-tuple-element.398, s32[32]{0:T(128)S(1)} %get-tuple-element.375, f32[32,128,256]{2,1,0:T(8,128)} %fusion.35), kind=kCustom, calls=%fused_computation.2.clone.1 | custom fusion | flops 1048576 | bytes 12583040 | tf_op jit(solution)/shard_map/while/body/eval_jaxpr/scatter-add | solution.py:42
  89.7 10.0 %scatter_fusion = f32[32,128,256]{2,1,0:T(8,128)} fusion(f32[32,128,256]{2,1,0:T(8,128)} %get-tuple-element.398, s32[32]{0:T(128)S(1)} %get-tuple-element.375, f32[32,128,256]{2,1,0:T(8,128)} %fusion.35), kind=kCustom, calls=%fused_computation.2.clone.1 | custom fusion | flops 1048576 | bytes 12583040 | tf_op jit(solution)/shard_map/while/body/eval_jaxpr/scatter-add | solution.py:42
  106.7 9.8 %scatter_fusion = f32[32,128,256]{2,1,0:T(8,128)} fusion(f32[32,128,256]{2,1,0:T(8,128)} %get-tuple-element.398, s32[32]{0:T(128)S(1)} %get-tuple-element.375, f32[32,128,256]{2,1,0:T(8,128)} %fusion.35), kind=kCustom, calls=%fused_computation.2.clone.1 | custom fusion | flops 1048576 | bytes 12583040 | tf_op jit(solution)/shard_map/while/body/eval_jaxpr/scatter-add | solution.py:42
  123.5 9.9 %scatter_fusion = f32[32,128,256]{2,1,0:T(8,128)} fusion(f32[32,128,256]{2,1,0:T(8,128)} %get-tuple-element.398, s32[32]{0:T(128)S(1)} %get-tuple-element.375, f32[32,128,256]{2,1,0:T(8,128)} %fusion.35), kind=kCustom, calls=%fused_computation.2.clone.1 | custom fusion | flops 1048576 | bytes 12583040 | tf_op jit(solution)/shard_map/while/body/eval_jaxpr/scatter-add | solution.py:42
  140.6 9.8 %scatter_fusion = f32[32,128,256]{2,1,0:T(8,128)} fusion(f32[32,128,256]{2,1,0:T(8,128)} %get-tuple-element.398, s32[32]{0:T(128)S(1)} %get-tuple-element.375, f32[32,128,256]{2,1,0:T(8,128)} %fusion.35), kind=kCustom, calls=%fused_computation.2.clone.1 | custom fusion | flops 1048576 | bytes 12583040 | tf_op jit(solution)/shard_map/while/body/eval_jaxpr/scatter-add | solution.py:42
  157.5 10.0 %scatter_fusion = f32[32,128,256]{2,1,0:T(8,128)} fusion(f32[32,128,256]{2,1,0:T(8,128)} %get-tuple-element.398, s32[32]{0:T(128)S(1)} %get-tuple-element.375, f32[32,128,256]{2,1,0:T(8,128)} %fusion.35), kind=kCustom, calls=%fused_computation.2.clone.1 | custom fusion | flops 1048576 | bytes 12583040 | tf_op jit(solution)/shard_map/while/body/eval_jaxpr/scatter-add | solution.py:42
  174.5 10.1 %scatter_fusion = f32[32,128,256]{2,1,0:T(8,128)} fusion(f32[32,128,256]{2,1,0:T(8,128)} %get-tuple-element.398, s32[32]{0:T(128)S(1)} %get-tuple-element.375, f32[32,128,256]{2,1,0:T(8,128)} %fusion.35), kind=kCustom, calls=%fused_computation.2.clone.1 | custom fusion | flops 1048576 | bytes 12583040 | tf_op jit(solution)/shard_map/while/body/eval_jaxpr/scatter-add | solution.py:42
  191.7 9.9 %scatter_fusion = f32[32,128,256]{2,1,0:T(8,128)} fusion(f32[32,128,256]{2,1,0:T(8,128)} %get-tuple-element.398, s32[32]{0:T(128)S(1)} %get-tuple-element.375, f32[32,128,256]{2,1,0:T(8,128)} %fusion.35), kind=kCustom, calls=%fused_computation.2.clone.1 | custom fusion | flops 1048576 | bytes 12583040 | tf_op jit(solution)/shard_map/while/body/eval_jaxpr/scatter-add | solution.py:42
  201.6 3.8 convert_element_type.63
  207.2 57.5 %reduce-scatter.3.cloned.1.call-done = bf16[256,256]{1,0:T(8,128)(2,1)} async-done(((bf16[4096,256]{1,0:T(8,128)(2,1)}), bf16[256,256]{1,0:T(8,128)(2,1)}) %reduce-scatter.3.cloned.1.call-update) | async-done | bytes 131088 | tf_op jit(solution)/shard_map/reduce_scatter | solution.py:56
  266.6 38.7 %all-gather.5.cloned.1.call-done = bf16[4096,256]{1,0:T(8,128)(2,1)} async-done(((bf16[256,256]{1,0:T(8,128)(2,1)}), bf16[4096,256]{1,0:T(8,128)(2,1)}) %all-gather.5.cloned.1.call-update) | async-done | bytes 2097168 | tf_op jit(solution)/shard_map/all_gather | solution.py:73
  307.8 134.8 %while.27 = (s32[]{:T(128)}, f32[32,128,256]{2,1,0:T(8,128)}, s32[256]{0:T(256)S(1)}, s32[256,16,128]{2,1,0:T(8,128)}, s32[]{:T(128)}, /*index=5*/s32[256]{0:T(2...) while((s32[]{:T(128)}, f32[32,128,256]{2,1,0:T(8,128)}, ...), condition=%wide.region_8.9_spmd, body=%wide.region_6.0_spmd.sunk | while | flops 271582656 | bytes 23862704 | solution.py:46
  314.6 10.1 %scatter_fusion.1 = f32[32,128,256]{2,1,0:T(8,128)} fusion(f32[32,128,256]{2,1,0:T(8,128)} %get-tuple-element.431, s32[32]{0:T(128)S(1)} %get-tuple-element.384, f32[32,128,256]{2,1,0:T(8,128)} %fusion.38), kind=kCustom, calls=%fused_computation.3.clone.1 | custom fusion | flops 1048576 | bytes 12583040 | tf_op jit(solution)/shard_map/while/body/eval_jaxpr/scatter-add | solution.py:42
  331.7 9.8 %scatter_fusion.1 = f32[32,128,256]{2,1,0:T(8,128)} fusion(f32[32,128,256]{2,1,0:T(8,128)} %get-tuple-element.431, s32[32]{0:T(128)S(1)} %get-tuple-element.384, f32[32,128,256]{2,1,0:T(8,128)} %fusion.38), kind=kCustom, calls=%fused_computation.3.clone.1 | custom fusion | flops 1048576 | bytes 12583040 | tf_op jit(solution)/shard_map/while/body/eval_jaxpr/scatter-add | solution.py:42
  348.4 10.0 %scatter_fusion.1 = f32[32,128,256]{2,1,0:T(8,128)} fusion(f32[32,128,256]{2,1,0:T(8,128)} %get-tuple-element.431, s32[32]{0:T(128)S(1)} %get-tuple-element.384, f32[32,128,256]{2,1,0:T(8,128)} %fusion.38), kind=kCustom, calls=%fused_computation.3.clone.1 | custom fusion | flops 1048576 | bytes 12583040 | tf_op jit(solution)/shard_map/while/body/eval_jaxpr/scatter-add | solution.py:42
  365.2 9.9 %scatter_fusion.1 = f32[32,128,256]{2,1,0:T(8,128)} fusion(f32[32,128,256]{2,1,0:T(8,128)} %get-tuple-element.431, s32[32]{0:T(128)S(1)} %get-tuple-element.384, f32[32,128,256]{2,1,0:T(8,128)} %fusion.38), kind=kCustom, calls=%fused_computation.3.clone.1 | custom fusion | flops 1048576 | bytes 12583040 | tf_op jit(solution)/shard_map/while/body/eval_jaxpr/scatter-add | solution.py:42
  382.0 9.8 %scatter_fusion.1 = f32[32,128,256]{2,1,0:T(8,128)} fusion(f32[32,128,256]{2,1,0:T(8,128)} %get-tuple-element.431, s32[32]{0:T(128)S(1)} %get-tuple-element.384, f32[32,128,256]{2,1,0:T(8,128)} %fusion.38), kind=kCustom, calls=%fused_computation.3.clone.1 | custom fusion | flops 1048576 | bytes 12583040 | tf_op jit(solution)/shard_map/while/body/eval_jaxpr/scatter-add | solution.py:42
  398.7 10.1 %scatter_fusion.1 = f32[32,128,256]{2,1,0:T(8,128)} fusion(f32[32,128,256]{2,1,0:T(8,128)} %get-tuple-element.431, s32[32]{0:T(128)S(1)} %get-tuple-element.384, f32[32,128,256]{2,1,0:T(8,128)} %fusion.38), kind=kCustom, calls=%fused_computation.3.clone.1 | custom fusion | flops 1048576 | bytes 12583040 | tf_op jit(solution)/shard_map/while/body/eval_jaxpr/scatter-add | solution.py:42
  415.6 10.1 %scatter_fusion.1 = f32[32,128,256]{2,1,0:T(8,128)} fusion(f32[32,128,256]{2,1,0:T(8,128)} %get-tuple-element.431, s32[32]{0:T(128)S(1)} %get-tuple-element.384, f32[32,128,256]{2,1,0:T(8,128)} %fusion.38), kind=kCustom, calls=%fused_computation.3.clone.1 | custom fusion | flops 1048576 | bytes 12583040 | tf_op jit(solution)/shard_map/while/body/eval_jaxpr/scatter-add | solution.py:42
  432.6 10.0 %scatter_fusion.1 = f32[32,128,256]{2,1,0:T(8,128)} fusion(f32[32,128,256]{2,1,0:T(8,128)} %get-tuple-element.431, s32[32]{0:T(128)S(1)} %get-tuple-element.384, f32[32,128,256]{2,1,0:T(8,128)} %fusion.38), kind=kCustom, calls=%fused_computation.3.clone.1 | custom fusion | flops 1048576 | bytes 12583040 | tf_op jit(solution)/shard_map/while/body/eval_jaxpr/scatter-add | solution.py:42
  447.0 76.9 %reduce-scatter.5.cloned.1.call-done = bf16[256,256]{1,0:T(8,128)(2,1)} async-done(((bf16[4096,256]{1,0:T(8,128)(2,1)}), bf16[256,256]{1,0:T(8,128)(2,1)}) %reduce-scatter.5.cloned.1.call-update) | async-done | bytes 131088 | tf_op jit(solution)/shard_map/reduce_scatter | solution.py:77
  526.6 94.1 %all-reduce.5.cloned.1.call-done = f32[256,256]{1,0:T(8,128)} async-done(((f32[256,256]{1,0:T(8,128)}), f32[256,256]{1,0:T(8,128)}) %all-reduce.5.cloned.1.call-update) | async-done | bytes 262160 | tf_op jit(solution)/shard_map/psum | solution.py:98
  (162 shorter events, 129.4 us)
Async XLA Ops:
  7.2 516.7 %copy-start = (bf16[256,256]{1,0:T(8,128)(2,1)S(1)}, bf16[256,256]{1,0:T(8,128)(2,1)}, u32[]{:S(2)}) copy-start(bf16[256,256]{1,0:T(8,128)(2,1)} %param.15) | copy-start | bytes 393220
  7.2 55.9 %all-gather.3.cloned.1.call-start = ((), (), s32[]{:S(2)}) async-start(), calls=%async_computation.2 | async-start | bytes 2228224 | tf_op jit(solution)/shard_map/all_gather | solution.py:52
  7.9 256.7 %reduce-scatter.3.cloned.1.call-start = ((), (), s32[]{:S(2)}) async-start(), calls=%async_computation.3 | async-start | bytes 2228224 | tf_op jit(solution)/shard_map/reduce_scatter | solution.py:56
  63.1 2.5 copy-start.2
  63.1 2.5 copy-start.3
  205.4 0.7 copy-start.4
  205.4 0.9 copy-start.1
  205.5 99.9 %all-gather.5.cloned.1.call-start = ((), (), s32[]{:S(2)}) async-start(), calls=%async_computation.6 | async-start | bytes 2228224 | tf_op jit(solution)/shard_map/all_gather | solution.py:73
  207.1 239.4 %all-reduce.3.cloned.1.call-start = ((), (), s32[]{:S(2)}) async-start(), calls=%async_computation.4 | async-start | bytes 524288 | tf_op jit(solution)/shard_map/psum | solution.py:98
  266.6 257.3 %reduce-scatter.5.cloned.1.call-start = ((), (), s32[]{:S(2)}) async-start(), calls=%async_computation.7 | async-start | bytes 2228224 | tf_op jit(solution)/shard_map/reduce_scatter | solution.py:77
  446.4 79.3 %copy-start.5 = (bf16[256,256]{1,0:T(8,128)(2,1)S(1)}, bf16[256,256]{1,0:T(8,128)(2,1)}, u32[]{:S(2)}) copy-start(bf16[256,256]{1,0:T(8,128)(2,1)} %reduce-scatter.3.cloned.1.call-done) | copy-start | bytes 393220
  446.5 174.2 %all-reduce.5.cloned.1.call-start = ((), (), s32[]{:S(2)}) async-start(), calls=%async_computation.5 | async-start | bytes 524288 | tf_op jit(solution)/shard_map/psum | solution.py:98
Sparse Core Ops, SparseCore 0:
  10.4 52.5 all-gather.2
  205.6 59.0 reduce-scatter.2
  267.1 38.2 all-gather.4
  308.1 106.7 all-reduce.2
  446.6 77.2 reduce-scatter.4
  526.9 93.6 all-reduce.4
